TPU v7x, 512 devices: a whole 4x4x16 slice. The times are simulated.
512 devices in a mesh: grp: 64 (over z, y), seq: 8 (over x, core).
Axes of the slice: x: 4, y: 4, z: 16, core: 2. Of those that a mesh axis runs over, the one named last changes fastest.
Arguments:
- tokens: bfloat16 [64, 1024, 2048], P('grp', 'seq'), may hold values from -6 to 6
- seg_ids: int32 [64, 1024], P('grp'), may hold values from 0 to 3, never falling along the last dimension, each value on 1 to 512 neighbouring positions
- deal: int32 [64, 1024], P('grp'), may hold values from 0 to 1023, each once within a row
- page_table: int32 [64, 128], P('grp'), may hold values from 0 to 127, each once within a row
- in_gain: float32 [2048], replicated, may hold values from 0.1 to 1.9
- w_query: bfloat16 [2048, 2048], P('grp', 'seq'), may hold values from -0.125 to 0.125
- key_projection_weight: bfloat16 [2048, 512], P('grp'), may hold values from -0.125 to 0.125
- value_projection_weight: bfloat16 [2048, 512], P('grp'), may hold values from -0.125 to 0.125
- q_gain: float32 [256], replicated, may hold values from 1.25 to 3.75
- key_norm_gain: float32 [256], replicated, may hold values from 0.1 to 1.9
- w_out: bfloat16 [2048, 2048], P('seq', 'grp'), may hold values from -0.125 to 0.125
- post_gain: float32 [2048], replicated, may hold values from 0.1 to 1.9
- final_gain: float32 [2048], replicated, may hold values from 0.1 to 1.9
- embed: bfloat16 [262144, 2048], P(('grp', 'seq')), may hold values from -0.375 to 0.375
Outputs:
- hidden_out: bfloat16 [64, 1024, 2048], P('grp', 'seq')
- kv_cache: bfloat16 [64, 128, 8, 1024], P('grp', 'seq')
- last_norm: float32 [256], replicated
- max_logit: float32 [256], replicated
Inputs may be any that keep to these rules, and one draw needn't show every extreme that they name: `seg_ids`: along each pack the prompt numbers never fall; every one of the 4 prompts occurs, none has more than 512 positions, and one has exactly that many. Each row of deal holds every packed position once. Each row of page_table holds every page of the pack once.
All inputs are finite; a program needn't handle non-finite values.
Results may differ from a plain program's by a relative error of at most 0.015.
The roundings to bfloat16 on the way count: a program that leaves them out, or rounds other values in their place, can miss the bound.
Values may be sent and summed in bfloat16 or wider, within the bound.
A program may use at most 64 MiB of HBM per device.

v0:
```python
import jax
import jax.numpy as jnp
from jax import lax
from jax.sharding import PartitionSpec as P

QUERY_HEADS = 8
KEY_HEADS = 2
PAGE_SLOTS = 8
SEGS = 4
eps = 1e-06
rope_base = 1000000.0
cap_value = 30.0


def rows_scaled(value_rows, scales):
    mean_square = jnp.mean(value_rows * value_rows, axis=-1, keepdims=True)
    return value_rows * lax.rsqrt(mean_square + eps) * scales


def rotate(value_rows, offsets):
    half_width = value_rows.shape[-1] // 2
    frequency = rope_base ** (
        -2.0 * jnp.arange(half_width, dtype=jnp.float32) / value_rows.shape[-1]
    )
    angles = offsets.astype(jnp.float32)[:, None] * frequency[None, :]
    cosine = jnp.cos(angles)[:, None, :]
    sine_table = jnp.sin(angles)[:, None, :]
    lower_half = value_rows[..., :half_width]
    upper_half = value_rows[..., half_width:]
    return jnp.concatenate(
        [
            lower_half * cosine - upper_half * sine_table,
            upper_half * cosine + lower_half * sine_table,
        ],
        axis=-1,
    )


def layout(segment, dealing):
    row_seg = jnp.take(segment, dealing)
    before = jnp.sum((segment[None, :] < row_seg[:, None]).astype(jnp.int32), axis=1)
    return (row_seg, dealing - before)


def attend(query, key_selected, value_selected, row_seg, dealing):
    scores = jnp.einsum("qhd,khd->hqk", query, key_selected, preferred_element_type=jnp.float32)
    allowed = (row_seg[:, None] == row_seg[None, :]) & (dealing[None, :] <= dealing[:, None])
    masked = jnp.where(allowed[None], scores, -1e30)
    row_peak = jnp.max(masked, axis=-1, keepdims=True)
    raw_weights = jnp.where(allowed[None], jnp.exp(masked - row_peak), 0.0)
    row_total = jnp.sum(raw_weights, axis=-1, keepdims=True)
    weights = (raw_weights / row_total).astype(jnp.bfloat16)
    attended = jnp.einsum(
        "hqk,khd->qhd", weights, value_selected, preferred_element_type=jnp.float32
    )
    return attended.astype(jnp.bfloat16).reshape(query.shape[0], -1)


def shards(
    tokens,
    seg_ids,
    deal,
    page_table,
    in_gain,
    w_query,
    key_projection_weight,
    value_projection_weight,
    q_gain,
    key_norm_gain,
    w_out,
    post_gain,
    final_gain,
    embed,
):
    own_tokens = tokens[0]
    rows_dev = own_tokens.shape[0]
    segment = seg_ids[0]
    dealing = deal[0]
    width_of_head = q_gain.shape[0]
    heads_local = w_query.shape[1] // width_of_head
    sequence_index = lax.axis_index("seq")
    own_start = sequence_index * rows_dev
    row_seg, offsets = layout(segment, dealing)
    normed_own = rows_scaled(own_tokens.astype(jnp.float32), in_gain).astype(jnp.bfloat16)
    normed_all = lax.all_gather(normed_own, "seq", axis=0, tiled=True)
    rows_of_pack = normed_all.shape[0]
    key_value_offsets = lax.dynamic_slice_in_dim(offsets, own_start, rows_dev, 0)
    query_full, key_full, value_full, out_full = (
        lax.all_gather(w_query, "grp", axis=0, tiled=True),
        lax.all_gather(key_projection_weight, "grp", axis=0, tiled=True),
        lax.all_gather(value_projection_weight, "grp", axis=0, tiled=True),
        lax.all_gather(w_out, "grp", axis=1, tiled=True),
    )
    query_raw = jnp.dot(normed_all, query_full, preferred_element_type=jnp.float32)
    key_unnormed = jnp.dot(normed_own, key_full, preferred_element_type=jnp.float32)
    value_unnormed = jnp.dot(normed_own, value_full, preferred_element_type=jnp.float32)
    query = rotate(
        rows_scaled(query_raw.reshape(rows_of_pack, heads_local, width_of_head), q_gain), offsets
    ).astype(jnp.bfloat16)
    rows_of_source = normed_own.shape[0]
    key_local_part = rotate(
        rows_scaled(key_unnormed.reshape(rows_of_source, KEY_HEADS, width_of_head), key_norm_gain),
        key_value_offsets,
    ).astype(jnp.bfloat16)
    value_local_part = rows_scaled(
        value_unnormed.reshape(rows_of_source, KEY_HEADS, width_of_head), 1.0
    ).astype(jnp.bfloat16)
    key_local_part = key_local_part.reshape(rows_of_source, KEY_HEADS * width_of_head)
    value_local_part = value_local_part.reshape(rows_of_source, KEY_HEADS * width_of_head)
    key_gathered, value_gathered = (
        lax.all_gather(key_local_part, "seq", axis=0, tiled=True),
        lax.all_gather(value_local_part, "seq", axis=0, tiled=True),
    )
    index_of_head = (sequence_index * heads_local + jnp.arange(heads_local, dtype=jnp.int32)) // (
        QUERY_HEADS // KEY_HEADS
    )
    key_selected = jnp.take(
        key_gathered.reshape(rows_of_pack, KEY_HEADS, width_of_head), index_of_head, axis=1
    )
    value_selected = jnp.take(
        value_gathered.reshape(rows_of_pack, KEY_HEADS, width_of_head), index_of_head, axis=1
    )
    attended = attend(query, key_selected, value_selected, row_seg, dealing)
    partial_out = jnp.dot(attended, out_full, preferred_element_type=jnp.float32)
    summed = lax.psum_scatter(
        partial_out.astype(jnp.bfloat16), "seq", scatter_dimension=0, tiled=True
    ).astype(jnp.float32)
    hidden = (own_tokens.astype(jnp.float32) + rows_scaled(summed, post_gain)).astype(jnp.bfloat16)
    inverse_assignment = jnp.argsort(dealing)
    inverse_page = jnp.argsort(page_table[0])
    own_pages = rows_dev // PAGE_SLOTS
    physical = sequence_index * own_pages + jnp.arange(own_pages, dtype=jnp.int32)
    logical_index = jnp.take(inverse_page, physical)
    packed = logical_index[:, None] * PAGE_SLOTS + jnp.arange(PAGE_SLOTS, dtype=jnp.int32)[None, :]
    source_index = jnp.take(inverse_assignment, packed.reshape(-1))
    stacked_rows = jnp.concatenate([key_gathered, value_gathered], axis=1)
    cache_pages = jnp.take(stacked_rows, source_index, axis=0).reshape(
        own_pages, PAGE_SLOTS, stacked_rows.shape[1]
    )
    last_pos = (
        jnp.sum(
            (segment[None, :] <= jnp.arange(SEGS, dtype=jnp.int32)[:, None]).astype(jnp.int32),
            axis=1,
        )
        - 1
    )
    local_row = jnp.take(inverse_assignment, last_pos) - own_start
    selector = (local_row[:, None] == jnp.arange(rows_dev, dtype=jnp.int32)[None, :]).astype(
        jnp.bfloat16
    )
    group_states = jnp.dot(selector, hidden, preferred_element_type=jnp.float32)
    pack_states = lax.psum(group_states.astype(jnp.bfloat16), "seq")
    states = lax.all_gather(pack_states, "grp", axis=0, tiled=True).astype(jnp.float32)
    last_norm = jnp.sqrt(jnp.mean(states * states, axis=-1))
    final = rows_scaled(states, final_gain).astype(jnp.bfloat16)
    logits = lax.dot_general(
        final, embed, (((1,), (1,)), ((), ())), preferred_element_type=jnp.float32
    )
    shard_max = jnp.max(cap_value * jnp.tanh(logits / cap_value), axis=1)
    max_logit = lax.pmax(shard_max, ("grp", "seq"))
    return (hidden[None], cache_pages[None], last_norm, max_logit)


def solution(mesh):
    return jax.shard_map(
        shards,
        mesh=mesh,
        in_specs=(
            P("grp", "seq", None),
            P("grp", None),
            P("grp", None),
            P("grp", None),
            P(),
            P("grp", "seq"),
            P("grp", None),
            P("grp", None),
            P(),
            P(),
            P("seq", "grp"),
            P(),
            P(),
            P(("grp", "seq"), None),
        ),
        out_specs=(P("grp", "seq", None), P("grp", "seq", None, None), P(), P()),
        check_vma=False,
    )
```

profile of v0, /device:TPU:1, one launch (start us, length us, event | category | flops | bytes accessed | tf_op | source)
XLA Modules:
  0.0 1011.3 jit_solution(3232940448721086610)
XLA Ops:
  7.3 0.7 all-gather.18.cloned.1.call-update
  8.0 0.7 all-gather.10.cloned.1.call-update
  8.7 0.7 compare_select_fusion.1
  9.5 5.7 gather_fusion
  16.3 132.1 %all-gather.18.cloned.1.call-done = bf16[2048,512]{1,0:T(8,128)(2,1)} async-done(((bf16[32,512]{1,0:T(8,128)(2,1)}), bf16[2048,512]{1,0:T(8,128)(2,1)}) %all-gather.18.cloned.1.call-update) | async-done | bytes 2097168 | tf_op jit(solution)/shard_map/all_gather | solution.py:90
  148.5 3.9 copy.40
  152.4 2.5 multiply_reduce_fusion.2
  155.2 0.8 copy.42
  156.1 132.3 %all-gather.10.cloned.1.call-done = bf16[2048,512]{1,0:T(8,128)(2,1)} async-done(((bf16[32,512]{1,0:T(8,128)(2,1)}), bf16[2048,512]{1,0:T(8,128)(2,1)}) %all-gather.10.cloned.1.call-update) | async-done | bytes 2097168 | tf_op jit(solution)/shard_map/all_gather | solution.py:91
  288.4 4.0 copy.36
  292.4 2.5 multiply_reduce_fusion.3
  295.1 0.8 copy.38
  296.6 1.0 fusion.15
  297.6 0.7 all-gather.22.cloned.1.call-update
  298.6 29.0 %all-gather.20.cloned.1.call-done = bf16[1024,512]{1,0:T(8,128)(2,1)} async-done(((bf16[128,512]{1,0:T(8,128)(2,1)}), bf16[1024,512]{1,0:T(8,128)(2,1)}) %all-gather.20.cloned.1.call-update) | async-done | bytes 1048592 | tf_op jit(solution)/shard_map/all_gather | solution.py:111
  327.6 2.2 reshape.529
  329.8 3.3 constant_dynamic-slice_fusion
  333.1 27.5 %all-gather.12.cloned.1.call-done = bf16[1024,512]{1,0:T(8,128)(2,1)} async-done(((bf16[128,512]{1,0:T(8,128)(2,1)}), bf16[1024,512]{1,0:T(8,128)(2,1)}) %all-gather.12.cloned.1.call-update) | async-done | bytes 1048592 | tf_op jit(solution)/shard_map/all_gather | solution.py:112
  360.6 2.2 reshape.527
  362.8 3.3 constant_dynamic-slice_fusion.1
  366.1 126.2 %all-gather.16.cloned.1.call-done = bf16[2048,256]{1,0:T(8,128)(2,1)} async-done(((bf16[32,256]{1,0:T(8,128)(2,1)}), bf16[2048,256]{1,0:T(8,128)(2,1)}) %all-gather.16.cloned.1.call-update) | async-done | bytes 1048592 | tf_op jit(solution)/shard_map/all_gather | solution.py:89
  492.3 48.3 %all-gather.14.cloned.1.call-done = bf16[1024,2048]{1,0:T(8,128)(2,1)} async-done(((bf16[128,2048]{1,0:T(8,128)(2,1)}), bf16[1024,2048]{1,0:T(8,128)(2,1)}) %all-gather.14.cloned.1.call-update) | async-done | bytes 4194320 | tf_op jit(solution)/shard_map/all_gather | solution.py:85
  540.6 3.9 multiply_reduce_fusion.1
  544.7 2.3 fusion.46
  547.0 1.0 fusion.1
  548.0 2.0 copy-done.3
  550.0 1.5 fusion.64
  551.5 121.2 %all-gather.22.cloned.1.call-done = bf16[256,2048]{0,1:T(8,128)(2,1)} async-done(((bf16[256,32]{0,1:T(8,128)(2,1)}), bf16[256,2048]{0,1:T(8,128)(2,1)}) %all-gather.22.cloned.1.call-update) | async-done | bytes 1048592 | tf_op jit(solution)/shard_map/all_gather | solution.py:92
  672.7 7.6 convolution_convert_fusion
  680.4 4.4 sort.35
  684.8 2.5 sort.34
  687.3 0.7 gather_fusion.1
  688.1 0.6 gather_fusion.4
  688.8 40.6 %reduce-scatter.2.cloned.1.call-done = bf16[128,2048]{1,0:T(8,128)(2,1)} async-done(((bf16[1024,2048]{1,0:T(8,128)(2,1)}), bf16[128,2048]{1,0:T(8,128)(2,1)}) %reduce-scatter.2.cloned.1.call-update) | async-done | bytes 524304 | tf_op jit(solution)/shard_map/reduce_scatter | solution.py:125
  729.4 1.2 fusion.11
  730.6 1.5 convolution_convert_fusion.1
  732.1 24.1 %psum.7 = bf16[4,2048]{1,0:T(4,128)(2,1)} all-reduce(bf16[4,2048]{1,0:T(4,128)(2,1)S(1)} %convolution_convert_fusion.1), channel_id=1, replica_groups=mesh['grp'=64,'seq'=8] {'seq'}, use_global_device_ids=true, to_apply=%region_12.14 | all-reduce | flops 8192 | bytes 32768 | tf_op jit(solution)/shard_map/psum | solution.py:152
  756.4 1.0 gather_fusion.2
  757.6 3.2 pad_maximum_fusion
  760.8 2.9 gather_fusion.3
  763.7 0.8 bitcast_select_fusion
  764.5 1.1 fusion.63
  765.5 121.9 %all-gather.24.cloned.1.call-done = bf16[64,4,2048]{2,1,0:T(4,128)(2,1)} async-done(((bf16[1,4,2048]{2,1,0:T(4,128)(2,1)}), bf16[64,4,2048]{2,1,0:T(4,128)(2,1)}) %all-gather.24.cloned.1.call-update) | async-done | bytes 1048592 | tf_op jit(solution)/shard_map/all_gather | solution.py:153
  887.5 2.5 reshape.630
  890.0 1.8 multiply_reduce_fusion
  891.8 0.6 add_rsqrt_fusion.1
  892.3 2.4 fusion.10
  894.8 110.0 %pmax.7 = f32[256]{0:T(256)} all-reduce(f32[256]{0:T(256)S(1)} %fusion.10), channel_id=1, replica_groups=mesh['grp'=64,'seq'=8] {'grp','seq'}, use_global_device_ids=true, to_apply=%region_15.17 | all-reduce | flops 256 | bytes 2048 | tf_op jit(solution)/shard_map/pmax | solution.py:160
  (78 shorter events, 3.6 us)
Async XLA Ops:
  7.2 885.2 %copy-start = (bf16[512,2048]{1,0:T(8,128)(2,1)S(1)}, bf16[512,2048]{1,0:T(8,128)(2,1)}, u32[]{:S(2)}) copy-start(bf16[512,2048]{1,0:T(8,128)(2,1)} %param.29) | copy-start | bytes 6291460
  7.2 8.0 copy-start.6
  7.2 8.1 copy-start.1
  7.2 8.6 copy-start.2
  7.2 141.2 %all-gather.18.cloned.1.call-start = ((), (), s32[]{:S(2)}) async-start(), calls=%async_computation.5 | async-start | bytes 2129920 | tf_op jit(solution)/shard_map/all_gather | solution.py:90
  7.9 280.5 %all-gather.10.cloned.1.call-start = ((), (), s32[]{:S(2)}) async-start(), calls=%async_computation.1 | async-start | bytes 2129920 | tf_op jit(solution)/shard_map/all_gather | solution.py:91
  8.7 318.9 %all-gather.20.cloned.1.call-start = ((), (), s32[]{:S(2)}) async-start(), calls=%async_computation.6 | async-start | bytes 1179648 | tf_op jit(solution)/shard_map/all_gather | solution.py:111
  9.4 143.0 %copy-start.7 = (f32[2048]{0:T(1024)S(1)}, f32[2048]{0:T(1024)}, u32[]{:S(2)}) copy-start(f32[2048]{0:T(1024)} %param.20) | copy-start | bytes 24580
  15.2 139.7 %copy-start.9 = (f32[256]{0:T(256)S(1)}, f32[256]{0:T(256)}, u32[]{:S(2)}) copy-start(f32[256]{0:T(256)} %param.25) | copy-start | bytes 3076
  156.0 204.6 %all-gather.12.cloned.1.call-start = ((), (), s32[]{:S(2)}) async-start(), calls=%async_computation.2 | async-start | bytes 1179648 | tf_op jit(solution)/shard_map/all_gather | solution.py:112
  295.9 196.3 %all-gather.16.cloned.1.call-start = ((), (), s32[]{:S(2)}) async-start(), calls=%async_computation.4 | async-start | bytes 1064960 | tf_op jit(solution)/shard_map/all_gather | solution.py:89
  296.5 244.1 %all-gather.14.cloned.1.call-start = ((), (), s32[]{:S(2)}) async-start(), calls=%async_computation.3 | async-start | bytes 4718592 | tf_op jit(solution)/shard_map/all_gather | solution.py:85
  297.6 375.1 %all-gather.22.cloned.1.call-start = ((), (), s32[]{:S(2)}) async-start(), calls=%async_computation.7 | async-start | bytes 1064960 | tf_op jit(solution)/shard_map/all_gather | solution.py:92
  298.3 431.1 %reduce-scatter.2.cloned.1.call-start = ((), (), s32[]{:S(2)}) async-start(), calls=%async_computation.8 | async-start | bytes 4718592 | tf_op jit(solution)/shard_map/reduce_scatter | solution.py:125
  366.1 178.5 %copy-start.10 = (f32[256]{0:T(256)S(1)}, f32[256]{0:T(256)}, u32[]{:S(2)}) copy-start(f32[256]{0:T(256)} %param.24) | copy-start | bytes 3076
  540.6 6.4 copy-start.5
  548.0 2.0 copy-start.3
  680.3 4.5 copy-start.12
  680.3 50.3 %copy-start.8 = (f32[2048]{0:T(1024)S(1)}, f32[2048]{0:T(1024)}, u32[]{:S(2)}) copy-start(f32[2048]{0:T(1024)} %param.27) | copy-start | bytes 24580
  680.3 207.2 %all-gather.24.cloned.1.call-start = ((), (), s32[]{:S(2)}) async-start(), calls=%async_computation.9 | async-start | bytes 1064960 | tf_op jit(solution)/shard_map/all_gather | solution.py:153
  730.6 33.9 %copy-start.4 = (bf16[128,2048]{1,0:T(8,128)(2,1)S(1)}, bf16[128,2048]{1,0:T(8,128)(2,1)}, u32[]{:S(2)}) copy-start(bf16[128,2048]{1,0:T(8,128)(2,1)} %reduce-scatter.2.cloned.1.call-done) | copy-start | bytes 1572868
  763.7 128.7 %copy-start.11 = (f32[2048]{0:T(1024)S(1)}, f32[2048]{0:T(1024)}, u32[]{:S(2)}) copy-start(f32[2048]{0:T(1024)} %param.28) | copy-start | bytes 24580
Sparse Core Ops, SparseCore 0:
  11.0 137.4 all-gather.17
  151.4 136.9 all-gather.9
  291.1 36.4 all-gather.19
  329.6 30.9 all-gather.11
  363.4 128.8 all-gather.15
  494.8 45.7 all-gather.13
  543.6 129.0 all-gather.21
  680.5 48.8 reduce-scatter.1
  756.3 131.0 all-gather.23
where the time goes:
time: 1010 us
  waiting for transfers between devices  782 us (77%)
  blocking collectives  134 us (13%)
  local copies, waits for them, and re-layouts  36.2 us (4%)
  other arithmetic  22.9 us (2%)
  matrix products  21.4 us (2%)
  between operations  14.2 us (1%)
    all_gather x1, waiting for transfers between devices, shards(): lax.all_gather(value_projection_weight, 'grp', axis=0, tiled=True)  132 us
    all_gather x1, waiting for transfers between devices, shards(): lax.all_gather(key_projection_weight, 'grp', axis=0, tiled=True)  132 us
    all_gather x1, waiting for transfers between devices, shards(): lax.all_gather(w_query, 'grp', axis=0, tiled=True)  126 us
    all_gather x1, waiting for transfers between devices, shards(): lax.all_gather(pack_states, 'grp', axis=0, tiled=True).astype(jnp.float32)  122 us
    all_gather x1, waiting for transfers between devices, shards(): lax.all_gather(w_out, 'grp', axis=1, tiled=True)  121 us
    pmax x1, blocking collectives, shards(): max_logit = lax.pmax(shard_max, ('grp', 'seq'))  110 us
    all_gather x1, waiting for transfers between devices, shards(): normed_all = lax.all_gather(normed_own, 'seq', axis=0, tiled=True)  48.3 us
    reduce_scatter x1, waiting for transfers between devices, shards(): lax.psum_scatter(partial_out.astype(jnp.bfloat16), 'seq', scatter_dimensi...  40.6 us
  transfers between devices with their start and end apart: 9, of which 9 were waited for; matrix products, arithmetic and copies ran while one was open for 6% of the time, Pallas kernels for 0%

commit v1 on v0

--- a/solution.py
+++ b/solution.py
@@ -88,7 +88,12 @@
     query_full, key_full, value_full, out_full = (
         lax.all_gather(w_query, "grp", axis=0, tiled=True),
         lax.all_gather(key_projection_weight, "grp", axis=0, tiled=True),
-        lax.all_gather(value_projection_weight, "grp", axis=0, tiled=True),
+        jnp.concatenate(
+            lax.all_to_all(
+                jnp.stack([value_projection_weight] * lax.axis_size("grp")), "grp", 0, 0
+            ),
+            axis=0,
+        ),
         lax.all_gather(w_out, "grp", axis=1, tiled=True),
     )
     query_raw = jnp.dot(normed_all, query_full, preferred_element_type=jnp.float32)

time: 1010 us -> 887 us (0.88)
  waiting for transfers between devices: 782 us -> 646 us
    all_gather x1 -> x0, waiting for transfers between devices: 132 us -> none  [shards(): lax.all_gather(value_projection_weight, 'grp', axis=0, tiled=True)]
    all_to_all x0 -> x1, waiting for transfers between devices: none -> 86.1 us  [shards(): lax.all_to_all(jnp.stack([value_projection_weight] * lax.axis_size('grp')...]
    all_gather x1, waiting for transfers between devices: 126 us -> 64.8 us  [shards(): lax.all_gather(w_query, 'grp', axis=0, tiled=True)]
    all_gather x1, waiting for transfers between devices: 29 us -> 0.02 us  [shards(): lax.all_gather(key_local_part, 'seq', axis=0, tiled=True)]
  transfers between devices with their start and end apart: 9 -> 9, of which waited for: 9 -> 8; matrix products, arithmetic and copies ran while one was open for 6% -> 6% of each run, Pallas kernels for 0% -> 0%
where the time goes in v1:
time: 887 us; the launch traced here: 886 us
  waiting for transfers between devices  646 us (73%)
  blocking collectives  134 us (15%)
  local copies, waits for them, and re-layouts  37.8 us (4%)
  other arithmetic  22.9 us (3%)
  matrix products  21.5 us (2%)
  between operations  14.6 us (2%)
  starting transfers between devices  9.58 us (1%)
    all_gather x1, waiting for transfers between devices, shards(): lax.all_gather(key_projection_weight, 'grp', axis=0, tiled=True)  133 us
    all_gather x1, waiting for transfers between devices, shards(): lax.all_gather(w_out, 'grp', axis=1, tiled=True)  126 us
    all_gather x1, waiting for transfers between devices, shards(): lax.all_gather(pack_states, 'grp', axis=0, tiled=True).astype(jnp.float32)  122 us
    pmax x1, blocking collectives, shards(): max_logit = lax.pmax(shard_max, ('grp', 'seq'))  110 us
    all_to_all x1, waiting for transfers between devices, shards(): lax.all_to_all(jnp.stack([value_projection_weight] * lax.axis_size('grp')...  86.1 us
    all_gather x1, waiting for transfers between devices, shards(): lax.all_gather(w_query, 'grp', axis=0, tiled=True)  64.8 us
    all_gather x1, waiting for transfers between devices, shards(): normed_all = lax.all_gather(normed_own, 'seq', axis=0, tiled=True)  48.3 us
    reduce_scatter x1, waiting for transfers between devices, shards(): lax.psum_scatter(partial_out.astype(jnp.bfloat16), 'seq', scatter_dimensi...  40.6 us
  transfers between devices with their start and end apart: 9, of which 8 were waited for; matrix products, arithmetic and copies ran while one was open for 6% of the time, Pallas kernels for 0%

profile of v1, /device:TPU:1, one launch (start us, length us, event | category | flops | bytes accessed | tf_op | source)
XLA Modules:
  0.0 885.9 jit_solution(2725317252822880056)
XLA Ops:
  7.3 0.7 all-gather.15.cloned.1.call-update
  8.0 0.7 compare_select_fusion.1
  8.7 5.7 gather_fusion
  15.6 132.9 %all-gather.15.cloned.1.call-done = bf16[2048,512]{1,0:T(8,128)(2,1)} async-done(((bf16[32,512]{1,0:T(8,128)(2,1)}), bf16[2048,512]{1,0:T(8,128)(2,1)}) %all-gather.15.cloned.1.call-update) | async-done | bytes 2097168 | tf_op jit(solution)/shard_map/all_gather | solution.py:90
  148.5 4.0 copy.40
  152.4 2.5 multiply_reduce_fusion.2
  155.3 0.8 copy.42
  156.1 0.7 all-gather.13.cloned.1.call-update
  156.8 1.6 stack.2
  158.4 9.1 %all-to-all-start = ((bf16[64,32,512]{2,1,0:T(8,128)(2,1)}), bf16[64,32,512]{2,1,0:T(8,128)(2,1)}, u32[]{:S(2)}, u32[]{:S(2)}) async-start(bf16[64,32,512]{2,1,0:T(8,128)(2,1)} %stack.2), calls=%async_computation | async-start | bytes 4194304 | tf_op jit(solution)/shard_map/all_to_all | solution.py:92
  167.6 1.0 fusion.15
  168.6 86.1 %all-to-all-done = bf16[64,32,512]{2,1,0:T(8,128)(2,1)} async-done(((bf16[64,32,512]{2,1,0:T(8,128)(2,1)}), bf16[64,32,512]{2,1,0:T(8,128)(2,1)}, u32[]{:S(2)}, u32[]{:S(2)}) %all-to-all-start) | async-done | bytes 2097184 | tf_op jit(solution)/shard_map/all_to_all | solution.py:92
  254.7 4.0 copy.36
  258.7 2.5 multiply_reduce_fusion.3
  261.5 0.8 copy.38
  263.1 2.2 reshape.535
  265.3 3.3 constant_dynamic-slice_fusion
  268.6 64.8 %all-gather.13.cloned.1.call-done = bf16[2048,256]{1,0:T(8,128)(2,1)} async-done(((bf16[32,256]{1,0:T(8,128)(2,1)}), bf16[2048,256]{1,0:T(8,128)(2,1)}) %all-gather.13.cloned.1.call-update) | async-done | bytes 1048592 | tf_op jit(solution)/shard_map/all_gather | solution.py:89
  333.5 48.3 %all-gather.11.cloned.1.call-done = bf16[1024,2048]{1,0:T(8,128)(2,1)} async-done(((bf16[128,2048]{1,0:T(8,128)(2,1)}), bf16[1024,2048]{1,0:T(8,128)(2,1)}) %all-gather.11.cloned.1.call-update) | async-done | bytes 4194320 | tf_op jit(solution)/shard_map/all_gather | solution.py:85
  381.8 3.9 multiply_reduce_fusion.1
  385.9 2.3 fusion.46
  388.2 1.0 fusion.1
  389.2 1.9 copy-done.3
  391.1 1.5 fusion.64
  392.6 22.4 %all-gather.9.cloned.1.call-done = bf16[1024,512]{1,0:T(8,128)(2,1)} async-done(((bf16[128,512]{1,0:T(8,128)(2,1)}), bf16[1024,512]{1,0:T(8,128)(2,1)}) %all-gather.9.cloned.1.call-update) | async-done | bytes 1048592 | tf_op jit(solution)/shard_map/all_gather | solution.py:117
  415.1 2.1 reshape.533
  417.2 3.3 constant_dynamic-slice_fusion.1
  420.5 126.2 %all-gather.19.cloned.1.call-done = bf16[256,2048]{0,1:T(8,128)(2,1)} async-done(((bf16[256,32]{0,1:T(8,128)(2,1)}), bf16[256,2048]{0,1:T(8,128)(2,1)}) %all-gather.19.cloned.1.call-update) | async-done | bytes 1048592 | tf_op jit(solution)/shard_map/all_gather | solution.py:97
  546.7 7.6 convolution_convert_fusion
  554.5 4.4 sort.35
  558.8 2.5 sort.34
  561.4 0.7 gather_fusion.1
  562.2 0.6 gather_fusion.4
  562.8 40.6 %reduce-scatter.2.cloned.1.call-done = bf16[128,2048]{1,0:T(8,128)(2,1)} async-done(((bf16[1024,2048]{1,0:T(8,128)(2,1)}), bf16[128,2048]{1,0:T(8,128)(2,1)}) %reduce-scatter.2.cloned.1.call-update) | async-done | bytes 524304 | tf_op jit(solution)/shard_map/reduce_scatter | solution.py:130
  603.5 1.2 fusion.11
  604.7 1.5 convolution_convert_fusion.1
  606.2 24.1 %psum.7 = bf16[4,2048]{1,0:T(4,128)(2,1)} all-reduce(bf16[4,2048]{1,0:T(4,128)(2,1)S(1)} %convolution_convert_fusion.1), channel_id=1, replica_groups=mesh['grp'=64,'seq'=8] {'seq'}, use_global_device_ids=true, to_apply=%region_12.14 | all-reduce | flops 8192 | bytes 32768 | tf_op jit(solution)/shard_map/psum | solution.py:157
  630.5 1.0 gather_fusion.2
  631.7 3.2 pad_maximum_fusion
  634.8 2.9 gather_fusion.3
  637.8 0.8 bitcast_select_fusion
  638.6 1.1 fusion.63
  639.6 122.1 %all-gather.21.cloned.1.call-done = bf16[64,4,2048]{2,1,0:T(4,128)(2,1)} async-done(((bf16[1,4,2048]{2,1,0:T(4,128)(2,1)}), bf16[64,4,2048]{2,1,0:T(4,128)(2,1)}) %all-gather.21.cloned.1.call-update) | async-done | bytes 1048592 | tf_op jit(solution)/shard_map/all_gather | solution.py:158
  761.7 2.5 reshape.636
  764.2 1.8 multiply_reduce_fusion
  766.0 0.6 add_rsqrt_fusion.1
  766.6 2.4 fusion.10
  769.0 110.0 %pmax.7 = f32[256]{0:T(256)} all-reduce(f32[256]{0:T(256)S(1)} %fusion.10), channel_id=1, replica_groups=mesh['grp'=64,'seq'=8] {'grp','seq'}, use_global_device_ids=true, to_apply=%region_15.17 | all-reduce | flops 256 | bytes 2048 | tf_op jit(solution)/shard_map/pmax | solution.py:165
  (80 shorter events, 3.6 us)
Async XLA Ops:
  7.2 759.4 %copy-start = (bf16[512,2048]{1,0:T(8,128)(2,1)S(1)}, bf16[512,2048]{1,0:T(8,128)(2,1)}, u32[]{:S(2)}) copy-start(bf16[512,2048]{1,0:T(8,128)(2,1)} %param.29) | copy-start | bytes 6291460
  7.2 7.3 copy-start.6
  7.2 7.3 copy-start.1
  7.2 7.9 copy-start.2
  7.2 141.2 %all-gather.15.cloned.1.call-start = ((), (), s32[]{:S(2)}) async-start(), calls=%async_computation.5 | async-start | bytes 2129920 | tf_op jit(solution)/shard_map/all_gather | solution.py:90
  7.9 255.2 %all-gather.17.cloned.1.call-start = ((), (), s32[]{:S(2)}) async-start(), calls=%async_computation.6 | async-start | bytes 1179648 | tf_op jit(solution)/shard_map/all_gather | solution.py:116
  8.7 143.7 %copy-start.8 = (f32[2048]{0:T(1024)S(1)}, f32[2048]{0:T(1024)}, u32[]{:S(2)}) copy-start(f32[2048]{0:T(1024)} %param.20) | copy-start | bytes 24580
  14.4 140.5 %copy-start.10 = (f32[256]{0:T(256)S(1)}, f32[256]{0:T(256)}, u32[]{:S(2)}) copy-start(f32[256]{0:T(256)} %param.25) | copy-start | bytes 3076
  148.5 8.4 copy-start.7
  156.1 177.4 %all-gather.13.cloned.1.call-start = ((), (), s32[]{:S(2)}) async-start(), calls=%async_computation.4 | async-start | bytes 1064960 | tf_op jit(solution)/shard_map/all_gather | solution.py:89
  158.4 96.3 %all-to-all-start = ((bf16[64,32,512]{2,1,0:T(8,128)(2,1)}), bf16[64,32,512]{2,1,0:T(8,128)(2,1)}, u32[]{:S(2)}, u32[]{:S(2)}) async-start(bf16[64,32,512]{2,1,0:T(8,128)(2,1)} %stack.2), calls=%async_computation | async-start | bytes 4194304 | tf_op jit(solution)/shard_map/all_to_all | solution.py:92
  167.5 214.3 %all-gather.11.cloned.1.call-start = ((), (), s32[]{:S(2)}) async-start(), calls=%async_computation.3 | async-start | bytes 4718592 | tf_op jit(solution)/shard_map/all_gather | solution.py:85
  168.6 246.5 %all-gather.9.cloned.1.call-start = ((), (), s32[]{:S(2)}) async-start(), calls=%async_computation.2 | async-start | bytes 1179648 | tf_op jit(solution)/shard_map/all_gather | solution.py:117
  262.3 284.5 %all-gather.19.cloned.1.call-start = ((), (), s32[]{:S(2)}) async-start(), calls=%async_computation.7 | async-start | bytes 1064960 | tf_op jit(solution)/shard_map/all_gather | solution.py:97
  262.8 340.6 %reduce-scatter.2.cloned.1.call-start = ((), (), s32[]{:S(2)}) async-start(), calls=%async_computation.8 | async-start | bytes 4718592 | tf_op jit(solution)/shard_map/reduce_scatter | solution.py:130
  268.6 117.1 %copy-start.11 = (f32[256]{0:T(256)S(1)}, f32[256]{0:T(256)}, u32[]{:S(2)}) copy-start(f32[256]{0:T(256)} %param.24) | copy-start | bytes 3076
  381.8 6.4 copy-start.5
  389.2 1.9 copy-start.3
  554.4 4.5 copy-start.13
  554.4 50.3 %copy-start.9 = (f32[2048]{0:T(1024)S(1)}, f32[2048]{0:T(1024)}, u32[]{:S(2)}) copy-start(f32[2048]{0:T(1024)} %param.27) | copy-start | bytes 24580
  554.4 207.3 %all-gather.21.cloned.1.call-start = ((), (), s32[]{:S(2)}) async-start(), calls=%async_computation.9 | async-start | bytes 1064960 | tf_op jit(solution)/shard_map/all_gather | solution.py:158
  604.7 33.9 %copy-start.4 = (bf16[128,2048]{1,0:T(8,128)(2,1)S(1)}, bf16[128,2048]{1,0:T(8,128)(2,1)}, u32[]{:S(2)}) copy-start(bf16[128,2048]{1,0:T(8,128)(2,1)} %reduce-scatter.2.cloned.1.call-done) | copy-start | bytes 1572868
  637.7 128.8 %copy-start.12 = (f32[2048]{0:T(1024)S(1)}, f32[2048]{0:T(1024)}, u32[]{:S(2)}) copy-start(f32[2048]{0:T(1024)} %param.28) | copy-start | bytes 24580
Sparse Core Ops, SparseCore 0:
  11.0 137.4 all-gather.14
  156.2 36.2 all-gather.16
  195.5 137.9 all-gather.12
  336.0 45.7 all-gather.10
  383.8 31.2 all-gather.8
  417.9 128.8 all-gather.18
  554.5 48.8 reduce-scatter.1
  630.4 131.2 all-gather.20
